TPU v7x, 32 devices: a whole 2x2x4 slice. The times are simulated.
32 devices in a mesh: groups: 2 (over x), tm: 16 (over z, y, core).
Axes of the slice: x: 2, y: 2, z: 4, core: 2. Of those that a mesh axis runs over, the one named last changes fastest.
Arguments:
- signal: float32 [2, 8192], P('groups', 'tm'), parts along dimension 0, may hold values from -6 to 6
- codes: bfloat16 [2, 1024, 8192], P('groups', None, 'tm'), parts along dimension 0, may hold values from -6 to 6
- dictionary: float32 [1024, 512], P('tm'), may hold values from -6 to 6
- thresholds: float32 [1024], replicated, may hold values from 0.02 to 0.2
Outputs:
- codes_out: bfloat16 [2, 1024, 8192], P('groups', None, 'tm'), parts along dimension 0
- dictionary_out: float32 [2048, 512], P(('groups', 'tm')), parts along dimension 0
- residual_out: float32 [2, 8192], P('groups', 'tm'), parts along dimension 0
There are 2 independent parts, one for each index of `groups`. A program takes and returns all parts, laid end to end along the dimension named above; an argument that names none is the same for every part. Nothing has to cross between parts.
All inputs are finite; a program needn't handle non-finite values.
Results may differ from a plain program's by a relative error of at most 0.0072.
Values may be sent and summed in bfloat16 or wider, within the bound.
A program may use at most 64 MiB of HBM per device.

v0:
```python
import functools

import jax
import jax.numpy as jnp
from jax import lax
from jax.experimental import pallas as pl
from jax.experimental.pallas import tpu as pltpu
from jax.sharding import PartitionSpec as P

ITERS = 2
CODE_STEP = 6.0
EPSILON = 1e-06
LANES = 128
MESH = pl.DeviceIdType.MESH
BF16, F32 = jnp.bfloat16, jnp.float32


PIECES = 2


def pieces_of(rows):
    return max(1, min(PIECES, rows // 16))


def rolled(x, shift):
    width = x.shape[1]
    shift = shift % width
    return x if shift == 0 else pltpu.roll(x, shift, 1)


def skew_total(lagged):
    lag_count, time_len = lagged.shape
    width = lag_count + time_len
    total = None
    for a in range(LANES // 8):
        part = None
        for b in range(lag_count // LANES):
            block = lagged[pl.ds(b * LANES + a * 8, 8), :]
            pieces = [block]
            if b:
                pieces.insert(0, jnp.zeros((8, b * LANES), F32))
            if width - b * LANES - time_len:
                pieces.append(jnp.zeros((8, width - b * LANES - time_len), F32))
            block = jnp.concatenate(pieces, axis=1)
            part = block if part is None else part + block
        part = rolled(part, 8 * a)
        total = part if total is None else total + part
    out = total[0:1, :]
    for r in range(1, 8):
        out = out + rolled(total, r)[r : r + 1, :]
    return out


def fill_frames(frames, extended):
    lag_count, time_len = frames.shape
    width = extended.shape[1]
    wide = jnp.broadcast_to(extended, (8, width))
    row = lax.broadcasted_iota(jnp.int32, (8, width), 0)
    base = wide
    for r in range(1, 8):
        base = jnp.where(row == r, rolled(wide, width - r), base)
    for a in range(LANES // 16):
        low, high = rolled(base, width - 16 * a), rolled(base, width - 16 * a - 8)
        both = jnp.concatenate([low, high], axis=0).astype(BF16)
        for b in range(lag_count // LANES):
            frames[pl.ds(b * LANES + a * 16, 16), :] = both[:, b * LANES : b * LANES + time_len]


def kernel(
    n, signal_hbm, codes_hbm, dictionary_hbm, thresholds_hbm,
    codes_out_hbm, atoms_ref, residual_ref,
    signal_ref, dictionary_ref, thresholds_ref, cutoffs, codes_b, current, atoms_b, lagged, frames, grad, keep,
    over_send, part_send, over_recv, part_recv, signal_next,
    core_send, core_recv, y_send, y_recv, z_send, z_recv,
    local_sem, halo_s, halo_r, sig_s, sig_r,
    az_s, az_r, ay_s, ay_r, ac_s, ac_r,
    gc_s, gc_r, gy_s, gy_r, gz_s, gz_r,
):
    rows, lag_count = dictionary_ref.shape
    atom_count, time_len = codes_b.shape
    factor = (atom_count * lag_count) ** (-0.5)
    nz = n // 4
    me = lax.axis_index("tm")
    core, y, z = me % 2, (me // 2) % 2, me // 4

    def index_of(zz, yy, cc):
        return (zz * 2 + yy) * 2 + cc

    partner = index_of(z, y, 1 - core)
    across = index_of(z, 1 - y, core)
    following, previous = (me + 1) % n, (me + n - 1) % n

    upper = (z * 2) // nz

    def layer_at(d):
        if d == nz - 1:
            return z
        fall, rise = nz - 1 - d, d
        fall = fall - (z - fall + nz) // nz
        rise = rise + (rise - z + nz) // nz
        return upper * rise + (1 - upper) * fall

    layers = [layer_at(d) for d in range(nz)]
    others = range(nz - 1)
    mine_at = nz - 1

    def copy_to(src, dst, send_sem, recv_sem, target):
        return pltpu.make_async_remote_copy(
            src_ref=src, dst_ref=dst, send_sem=send_sem, recv_sem=recv_sem,
            device_id={"tm": target}, device_id_type=MESH,
        )

    loads = [
        pltpu.make_async_copy(dictionary_hbm, dictionary_ref, local_sem.at[1]),
        pltpu.make_async_copy(signal_hbm, signal_ref, local_sem.at[2]),
        pltpu.make_async_copy(thresholds_hbm, thresholds_ref, local_sem.at[3]),
        pltpu.make_async_copy(codes_hbm.at[0], codes_b, local_sem.at[0]),
    ]
    for load in loads:
        load.start()

    barrier = pltpu.get_barrier_semaphore()
    for target in [partner, across, following, previous] + [index_of(layers[d], y, core) for d in others]:
        pl.semaphore_signal(barrier, inc=1, device_id={"tm": target}, device_id_type=MESH)
    pl.semaphore_wait(barrier, 4 + nz - 1)

    sent = []

    def start(copy):
        copy.start()
        sent.append(copy)

    def block(it, index):
        return atoms_b.at[it, pl.ds(pl.multiple_of(index * rows, rows), rows), :]

    pieces = pieces_of(rows)
    part = rows // pieces

    def gather(it):
        def move(index, q, send_sem, recv_sem, target):
            held = atoms_b.at[it, pl.ds(pl.multiple_of(index * rows + q * part, part), part), :]
            return copy_to(held, held, send_sem, recv_sem, target)

        def to_across(index, d, q):
            return move(index, q, ay_s.at[it, d, q], ay_r.at[it, d, q], across)

        def to_partner(index, d, e, q):
            return move(index, q, ac_s.at[it, d, e, q], ac_r.at[it, d, e, q], partner)

        for q in range(pieces):
            for d in others:
                start(move(me, q, az_s.at[it, d, q], az_r.at[it, z, q], index_of(layers[d], y, core)))
            start(to_across(me, mine_at, q))
        for q in range(pieces):
            start(to_partner(me, mine_at, 0, q))
        for q in range(pieces):
            for d in others:
                held = index_of(layers[d], y, core)
                move(held, q, az_s.at[it, d, q], az_r.at[it, layers[d], q], across).wait_recv()
                start(to_across(held, d, q))
                start(to_partner(held, d, 0, q))
        for q in range(pieces):
            held = index_of(z, 1 - y, core)
            to_across(held, mine_at, q).wait_recv()
            start(to_partner(held, mine_at, 1, q))
        for q in range(pieces):
            for d in others:
                held = index_of(layers[d], 1 - y, core)
                to_across(held, d, q).wait_recv()
                start(to_partner(held, d, 1, q))
        for d in range(nz):
            for e in range(2):
                for q in range(pieces):
                    held = index_of(layers[d], y if e == 0 else 1 - y, 1 - core)
                    to_partner(held, d, e, q).wait_recv()

    loads[0].wait()
    loads[1].wait()
    atoms_ref[...] = dictionary_ref[...]
    block(0, me)[...] = dictionary_ref[...].astype(BF16)
    signal_copy = copy_to(signal_ref, signal_next, sig_s, sig_r, previous)

    @pl.when(me > 0)
    def _():
        signal_copy.start()

    for it in range(ITERS):
        last = it == ITERS - 1
        gather(it)
        if it == 0:
            loads[2].wait()
            cutoffs[...] = CODE_STEP * jnp.broadcast_to(thresholds_ref[...], (8, atom_count)).T[:, 0:1]
            loads[3].wait()
        lagged[...] = lax.dot_general(
            atoms_b[it], codes_b[...], (((0,), (0,)), ((), ())), preferred_element_type=F32
        )
        summed = skew_total(lagged)
        mine, over = summed[:, :time_len], summed[:, time_len:]
        over_send[it] = over
        part_send[it] = mine
        over_copy = copy_to(over_send.at[it], over_recv.at[it], halo_s.at[it, 0], halo_r.at[it, 0], following)
        part_copy = copy_to(part_send.at[it], part_recv.at[it], halo_s.at[it, 1], halo_r.at[it, 1], previous)

        @pl.when(me < n - 1)
        def _():
            over_copy.start()

        @pl.when(me > 0)
        def _():
            part_copy.start()

        @pl.when(me > 0)
        def _():
            over_copy.wait_recv()

        @pl.when(me == 0)
        def _():
            over_recv[it] = jnp.zeros_like(over)

        @pl.when(me < n - 1)
        def _():
            part_copy.wait_recv()
            if it == 0:
                signal_copy.wait_recv()

        @pl.when(me == n - 1)
        def _():
            part_recv[it] = -over
            if it == 0:
                signal_next[...] = jnp.zeros_like(over)

        residual = signal_ref[...] - factor * (mine + over_recv[it])
        ahead = signal_next[...] - factor * (part_recv[it] + over)
        if last:
            residual_ref[...] = residual
        extended = jnp.concatenate([residual, ahead], axis=1).astype(BF16).astype(F32)
        fill_frames(frames, extended)

        order = range(nz)
        layer = 4 * rows

        def own(d, yy, cc):
            return grad[d, pl.ds(pl.multiple_of((yy * 2 + cc) * rows, rows), rows), :]

        core_copies, y_copies, z_copies = {}, {}, {}
        for d in order:
            picked = pl.ds(pl.multiple_of(layers[d] * layer, layer), layer)
            grad[d] = jnp.dot(codes_b[picked, :], frames[...], preferred_element_type=F32)
            core_send[it, d, 0] = own(d, y, 1 - core).astype(BF16)
            core_send[it, d, 1] = own(d, 1 - y, 1 - core).astype(BF16)
            core_copies[d] = copy_to(
                core_send.at[it, d], core_recv.at[it, d], gc_s.at[it, d], gc_r.at[it, d], partner
            )
            start(core_copies[d])
        step_rows = min(256, atom_count)
        steps = atom_count // step_rows

        def advance(i):
            picked = pl.ds(i * step_rows, step_rows)
            matched = jnp.dot(atoms_b[it, picked, :], frames[...], preferred_element_type=F32)
            before = codes_b[picked, :].astype(F32) if it == 0 else current[picked, :]
            shrink = before + (CODE_STEP * factor) * matched
            cutoff = cutoffs[picked, :]
            after = shrink - jnp.minimum(jnp.maximum(shrink, -cutoff), cutoff)
            if not last:
                current[picked, :] = after
            codes_b[picked, :] = after.astype(BF16)

        advance(0)
        for d in order:
            core_copies[d].wait_recv()
            y_send[it, d] = (own(d, 1 - y, core) + core_recv[it, d, 1].astype(F32)).astype(BF16)
            keep[d] = own(d, y, core) + core_recv[it, d, 0].astype(F32)
            y_copies[d] = copy_to(y_send.at[it, d], y_recv.at[it, d], gy_s.at[it, d], gy_r.at[it, d], across)
            start(y_copies[d])

        for i in range(1, steps - 1):
            advance(i)
        for d in order:
            y_copies[d].wait_recv()
            keep[d] = keep[d] + y_recv[it, d].astype(F32)
            if d != mine_at:
                z_send[it, d] = keep[d].astype(BF16)
                z_copies[d] = copy_to(
                    z_send.at[it, d], z_recv.at[it, z], gz_s.at[it, d], gz_r.at[it, z], index_of(layers[d], y, core)
                )
                start(z_copies[d])
        advance(steps - 1)
        if last:
            store = pltpu.make_async_copy(codes_b, codes_out_hbm.at[0], local_sem.at[1])
            store.start()
        total = keep[mine_at]
        for d in others:
            copy_to(
                z_send.at[it, d], z_recv.at[it, layers[d]], gz_s.at[it, d], gz_r.at[it, layers[d]], across
            ).wait_recv()
            total = total + z_recv[it, layers[d]].astype(F32)
        updated = atoms_ref[...] + factor * total
        fresh = updated / jnp.sqrt(jnp.mean(updated * updated, axis=1, keepdims=True) + EPSILON)
        atoms_ref[...] = fresh
        if not last:
            block(it + 1, me)[...] = fresh.astype(BF16)

        @pl.when(me < n - 1)
        def _():
            over_copy.wait_send()

        @pl.when(me > 0)
        def _():
            part_copy.wait_send()

    @pl.when(me > 0)
    def _():
        signal_copy.wait_send()

    for copy in sent:
        copy.wait_send()
    store.wait()


def on_device(n, signal, codes, dictionary, thresholds):
    _, atom_count, time_len = codes.shape
    rows, lag_count = dictionary.shape
    nz = n // 4
    vmem, dma = pltpu.VMEM, pltpu.SemaphoreType.DMA
    inside = pl.BlockSpec(memory_space=pltpu.VMEM)
    outside = pl.BlockSpec(memory_space=pltpu.HBM)
    piece = (rows, lag_count)
    made = tuple(
        pl.pallas_call(
            functools.partial(kernel, n),
            name="learn",
            out_shape=(
                jax.ShapeDtypeStruct(codes.shape, BF16),
                jax.ShapeDtypeStruct(piece, F32),
                jax.ShapeDtypeStruct(signal.shape, F32),
            ),
            in_specs=[outside] * 4,
            out_specs=(pl.BlockSpec(memory_space=pl.ANY), inside, inside),
            scratch_shapes=[
                vmem(signal.shape, F32),
                vmem(piece, F32),
                vmem((1, atom_count), F32),
                vmem((atom_count, 1), F32),
                vmem((atom_count, time_len), BF16),
                vmem((atom_count, time_len), F32),
                vmem((ITERS, atom_count, lag_count), BF16),
                vmem((lag_count, time_len), F32),
                vmem((lag_count, time_len), BF16),
                vmem((nz, 4 * rows, lag_count), F32),
                vmem((nz, *piece), F32),
                vmem((ITERS, 1, time_len), F32),
                vmem((ITERS, 1, time_len), F32),
                vmem((ITERS, 1, time_len), F32),
                vmem((ITERS, 1, time_len), F32),
                vmem((1, time_len), F32),
                vmem((ITERS, nz, 2, *piece), BF16),
                vmem((ITERS, nz, 2, *piece), BF16),
                vmem((ITERS, nz, *piece), BF16),
                vmem((ITERS, nz, *piece), BF16),
                vmem((ITERS, nz, *piece), BF16),
                vmem((ITERS, nz, *piece), BF16),
                dma((4,)),
                dma((ITERS, 2)),
                dma((ITERS, 2)),
                dma,
                dma,
                *[dma((ITERS, nz, pieces_of(rows)))] * 4,
                *[dma((ITERS, nz, 2, pieces_of(rows)))] * 2,
                *[dma((ITERS, nz))] * 6,
            ],
            compiler_params=pltpu.CompilerParams(
                collective_id=0, has_side_effects=True, vmem_limit_bytes=66_000_000
            ),
        )(signal, codes, dictionary, thresholds[None, :])
    )

    quarter = atom_count // 4

    def publish(codes_ref, atoms_ref, residual_ref, codes_out, atoms_out, residual_out, held, atoms, residual, sem_in, sem_out):
        views = [
            [ref.at[0, pl.ds(i * quarter, quarter), :] for ref in (codes_ref, held, codes_out)] for i in range(4)
        ] + [[atoms_ref, atoms, atoms_out], [residual_ref, residual, residual_out]]
        takes = [pltpu.make_async_copy(view[0], view[1], sem_in.at[i]) for i, view in enumerate(views)]
        puts = [pltpu.make_async_copy(view[1], view[2], sem_out.at[i]) for i, view in enumerate(views)]
        for take in takes:
            take.start()
        for take, put in zip(takes, puts):
            take.wait()
            put.start()
        for put in puts:
            put.wait()

    return tuple(
        pl.pallas_call(
            publish,
            name="publish",
            out_shape=tuple(jax.ShapeDtypeStruct(x.shape, x.dtype) for x in made),
            in_specs=[outside] * 3,
            out_specs=(outside,) * 3,
            scratch_shapes=[*[vmem(x.shape, x.dtype) for x in made], dma((6,)), dma((6,))],
        )(*made)
    )


def solution(mesh):
    return jax.shard_map(
        functools.partial(on_device, mesh.shape["tm"]),
        mesh=mesh,
        in_specs=(P("groups", "tm"), P("groups", None, "tm"), P("tm", None), P()),
        out_specs=(P("groups", None, "tm"), P(("groups", "tm"), None), P("groups", "tm")),
        check_vma=False,
    )
```

profile of v0, /device:TPU:0, one launch (start us, length us, event | category | flops | bytes accessed | tf_op | source)
XLA Modules:
  0.0 63.7 jit_solution(16795501529163376323)
XLA Ops:
  0.6 61.0 %learn.1 = (bf16[1,1024,512]{2,1,0:T(8,128)(2,1)}, f32[64,512]{1,0:T(8,128)}, f32[1,512]{1,0:T(1,128)}) custom-call(f32[1,512]{1,0:T(1,128)} %signal_hbm.1, bf16[1,1024,512]{2,1,0:T(8,128)(2,1)} %codes_hbm.1, f32[64,512]{1,0:T(8,128)} %dictionary_hbm.1, f32[1,1024]{1,0:T(1,128)} %bitcast.1), custom_call_target="tpu_custom_call" | custom-call | tf_op jit(solution)/shard_map/learn/pallas_call | solution.py:330
  61.6 2.1 %publish.1 = (bf16[1,1024,512]{2,1,0:T(8,128)(2,1)}, f32[64,512]{1,0:T(8,128)}, f32[1,512]{1,0:T(1,128)}) custom-call(bf16[1,1024,512]{2,1,0:T(8,128)(2,1)} %get-tuple-element.6.codes_ref, f32[64,512]{1,0:T(8,128)} %get-tuple-element.7.atoms_ref, f32[1,512]{1,0:T(1,128)} %get-tuple-element.8.residual_ref), custom_call_target="tpu_custom_call" | custom-call | tf_op jit(solution)/shard_map/publish/pallas_call | solution.py:395
where the time goes:
time: 63.8 us; the launch traced here: 63.7 us
  Pallas kernels  63.1 us (99%)
  between operations  0.64 us (1%)
    pallas_call x1, Pallas kernels, on_device(): pl.pallas_call(functools.partial(kernel, n), name='learn', out_shape=(jax...  61 us
    pallas_call x1, Pallas kernels, on_device(): pl.pallas_call(publish, name='publish', out_shape=tuple((jax.ShapeDtypeSt...  2.06 us

commit v1 on v0

v1 whole, which is shorter than its diff:
```python
import functools

import jax
import jax.numpy as jnp
from jax import lax
from jax.experimental import pallas as pl
from jax.experimental.pallas import tpu as pltpu
from jax.sharding import PartitionSpec as P

ITERS = 2
CODE_STEP = 6.0
EPSILON = 1e-06
LANES = 128
MESH = pl.DeviceIdType.MESH
BF16, F32 = jnp.bfloat16, jnp.float32
PIECES = 2


def pieces_of(rows):
    return max(1, min(PIECES, rows // 16))


def rolled(x, shift):
    width = x.shape[1]
    shift = shift % width
    return x if shift == 0 else pltpu.roll(x, shift, 1)


def skew_total(lagged):
    lag_count, time_len = lagged.shape
    width = lag_count + time_len
    total = None
    for a in range(LANES // 8):
        part = None
        for b in range(lag_count // LANES):
            block = lagged[pl.ds(b * LANES + a * 8, 8), :]
            pieces = [block]
            if b:
                pieces.insert(0, jnp.zeros((8, b * LANES), F32))
            if width - b * LANES - time_len:
                pieces.append(jnp.zeros((8, width - b * LANES - time_len), F32))
            block = jnp.concatenate(pieces, axis=1)
            part = block if part is None else part + block
        part = rolled(part, 8 * a)
        total = part if total is None else total + part
    out = total[0:1, :]
    for r in range(1, 8):
        out = out + rolled(total, r)[r : r + 1, :]
    return out


def fill_frames(frames, extended):
    lag_count = frames.shape[1]
    width = extended.shape[1]
    halves = frames.shape[0] // lag_count
    wide = jnp.broadcast_to(extended, (8, width))
    row = lax.broadcasted_iota(jnp.int32, (8, width), 0)
    base = wide
    for r in range(1, 8):
        base = jnp.where(row == r, rolled(wide, width - r), base)
    for a in range(LANES // 16):
        low, high = rolled(base, width - 16 * a), rolled(base, width - 16 * a - 8)
        both = jnp.concatenate([low, high], axis=0).astype(BF16)
        for half in range(halves):
            for b in range(lag_count // LANES):
                at = half * lag_count + b * LANES
                frames[pl.ds(at + a * 16, 16), :] = both[:, at : at + lag_count]


def kernel(
    n, signal_hbm, codes_hbm, dictionary_hbm, thresholds_hbm,
    codes_out, atoms_out, residual_out,
    atoms_ref, signal_ref, dictionary_ref, thresholds_ref, cutoffs_all, cutoffs, codes_b, current, atoms_b, lagged,
    frames, grad, keep, extended_ref, part_send, from_partner, from_previous, from_following,
    y_send, y_recv, z_send, z_recv,
    local_sem, send_sem, whole_r, halo_r, az_r, over_r, gy_r, gz_r,
):
    rows, lag_count = dictionary_ref.shape
    nz, _, _, width = codes_b.shape
    atom_count = 4 * nz * rows
    factor = (atom_count * lag_count) ** (-0.5)
    pieces = pieces_of(rows)
    part = rows // pieces
    me = lax.axis_index("tm")
    core, y, z = me % 2, (me // 2) % 2, me // 4
    chip, chips = me // 2, n // 2

    def index_of(zz, yy, cc):
        return (zz * 2 + yy) * 2 + cc

    partner = index_of(z, y, 1 - core)
    across = index_of(z, 1 - y, core)
    upper = (z * 2) // nz

    def layer_at(d):
        if d == nz - 1:
            return z
        fall, rise = nz - 1 - d, d
        fall = fall - (z - fall + nz) // nz
        rise = rise + (rise - z + nz) // nz
        return upper * rise + (1 - upper) * fall

    layers = [layer_at(d) for d in range(nz)]
    others = range(nz - 1)
    def copy_to(src, dst, send, recv_sem, target):
        return pltpu.make_async_remote_copy(
            src_ref=src, dst_ref=dst, send_sem=send_sem.at[send], recv_sem=recv_sem,
            device_id={"tm": target}, device_id_type=MESH,
        )

    def arrived(ref, recv_sem):
        pltpu.make_async_copy(ref, ref, recv_sem).wait()

    sent = []

    def start(copy, when=None):
        if when is None:
            copy.start()
        else:
            pl.when(when)(copy.start)
        sent.append((copy, when))

    def lanes_of(cc):
        return pl.ds(pl.multiple_of(cc * lag_count, LANES), lag_count)

    def slab(p):
        return pl.ds(p * part, part)

    own = lanes_of(core)
    loads = [
        pltpu.make_async_copy(dictionary_hbm, dictionary_ref, local_sem.at[0]),
        pltpu.make_async_copy(signal_hbm, signal_ref, local_sem.at[1]),
        pltpu.make_async_copy(thresholds_hbm, thresholds_ref, local_sem.at[2]),
        pltpu.make_async_copy(codes_hbm.at[:, :, core], codes_b.at[:, :, :, own], local_sem.at[3]),
    ]
    for load in loads:
        load.start()

    barrier = pltpu.get_barrier_semaphore()
    for target in [partner, across] + [index_of(layers[d], y, core) for d in others]:
        pl.semaphore_signal(barrier, inc=1, device_id={"tm": target}, device_id_type=MESH)

    loads[0].wait()
    atoms_ref[...] = dictionary_ref[...]
    atoms_b[0, z, y] = dictionary_ref[...].astype(BF16)
    pl.semaphore_wait(barrier, 2 + nz - 1)

    def piece(it, zz, yy, p):
        return atoms_b.at[it, zz, yy, slab(p), :]

    def along(it, zz, p, target):
        held = piece(it, zz, y, p)
        return copy_to(held, held, 0, az_r.at[zz, p], index_of(target, y, core))

    def over(it, zz, p):
        held = piece(it, zz, y, p)
        return copy_to(held, held, 1, over_r.at[0], across)

    def offer(it, p):
        for d in others:
            start(along(it, z, p, layers[d]))
        start(over(it, z, p))

    def landed(it, zz, p):
        arrived(piece(it, zz, y, p), az_r.at[zz, p])
        over(it, zz, p).start()

    def gather(it):
        for p in range(pieces):
            for hops in range(1, nz):
                pl.when(z - hops >= 0)(functools.partial(landed, it, z - hops, p))
                pl.when(z + hops < nz)(functools.partial(landed, it, z + hops, p))
            for d in others:
                sent.append((over(it, layers[d], p), None))
        theirs = atoms_b.at[it, :, 1 - y]
        arrived(theirs, over_r.at[0])

    for p in range(pieces):
        offer(0, p)
    start(copy_to(codes_hbm.at[:, :, 1 - core], codes_b.at[:, :, :, own], 2, whole_r.at[0], partner))
    loads[2].wait()
    cutoffs_all[...] = CODE_STEP * jnp.broadcast_to(thresholds_ref[...], (8, atom_count)).T[:, 0:1]
    for zz in range(nz):
        for yy in range(2):
            at = pl.multiple_of(index_of(zz, yy, core) * rows, rows)
            cutoffs[zz, yy] = cutoffs_all[pl.ds(at, rows), :]
    loads[1].wait()

    for it in range(ITERS):
        last = it == ITERS - 1
        gather(it)
        if it == 0:
            loads[3].wait()
            arrived(codes_b.at[:, :, :, lanes_of(1 - core)], whole_r.at[0])
        lagged[...] = lax.dot_general(
            atoms_b[it].reshape(2 * nz * rows, lag_count), codes_b[...].reshape(2 * nz * rows, width),
            (((0,), (0,)), ((), ())), preferred_element_type=F32,
        )
        part_send[it] = -factor * skew_total(lagged)
        part_send[it, :, own] += signal_ref[...]

        start(copy_to(part_send.at[it], from_partner.at[it], 3, halo_r.at[it, 0], partner))
        for cc in range(2):
            start(
                copy_to(
                    part_send.at[it, :, pl.ds(width, lag_count)], from_previous.at[it, core],
                    3, halo_r.at[it, 1], 2 * (chip + 1) + cc,
                ),
                chip < chips - 1,
            )
            start(
                copy_to(
                    part_send.at[it, :, pl.ds(0, lag_count)], from_following.at[it, core],
                    3, halo_r.at[it, 2], 2 * (chip - 1) + cc,
                ),
                chip > 0,
            )

        @pl.when(chip == 0)
        def _():
            from_previous[it] = jnp.zeros_like(from_previous[it])

        @pl.when(chip == chips - 1)
        def _():
            from_following[it] = jnp.zeros_like(from_following[it])

        arrived(from_partner.at[it], halo_r.at[it, 0])

        @pl.when(chip > 0)
        def _():
            arrived(from_previous.at[it], halo_r.at[it, 1])

        @pl.when(chip < chips - 1)
        def _():
            arrived(from_following.at[it], halo_r.at[it, 2])

        total = part_send[it] + from_partner[it]
        head = total[:, :lag_count] + (from_previous[it, 0] + from_previous[it, 1])
        tail = total[:, width:] + (from_following[it, 0] + from_following[it, 1])
        residual = jnp.concatenate([head, total[:, lag_count:width], tail], axis=1)
        lane = lax.broadcasted_iota(jnp.int32, residual.shape, 1)
        held = width + lag_count * jnp.minimum(chips - 1 - chip, 1)
        residual = jnp.where(lane < held, residual, 0.0)
        if last:
            extended_ref[...] = residual
            residual_store = pltpu.make_async_copy(extended_ref.at[:, own], residual_out, local_sem.at[1])
            residual_store.start()
        fill_frames(frames, residual.astype(BF16).astype(F32))

        order = range(nz)
        column = (nz * rows, width)
        crossing = jnp.dot(codes_b[:, 1 - y].reshape(column), frames[...], preferred_element_type=F32)
        y_send[it] = crossing.reshape(nz, rows, lag_count).astype(BF16)

        def y_copy(d, p):
            lay = layers[d]
            return copy_to(y_send.at[it, lay, slab(p), :], y_recv.at[it, lay, slab(p), :], 4, gy_r.at[d, p], across)

        def z_copy(lay, p):
            return copy_to(
                z_send.at[it, lay, slab(p), :], z_recv.at[it, z, slab(p), :], 5, gz_r.at[z, p], index_of(lay, y, core)
            )

        for p in range(pieces):
            for d in order:
                start(y_copy(d, p))
        grad[...] = jnp.dot(
            codes_b[:, y].reshape(column), frames[...], preferred_element_type=F32
        ).reshape(nz, rows, lag_count)

        def advance(yy, half):
            picked = pl.ds(half * lag_count, lag_count)
            matched = jnp.dot(
                atoms_b[it, :, yy].reshape(nz * rows, lag_count), frames[picked, :], preferred_element_type=F32
            )
            store = (slice(None), yy, slice(None), picked)
            before = codes_b[store].astype(F32) if it == 0 else current[store]
            shrink = before + (CODE_STEP * factor) * matched.reshape(nz, rows, lag_count)
            cutoff = cutoffs[:, yy]
            after = shrink - jnp.minimum(jnp.maximum(shrink, -cutoff), cutoff)
            if not last:
                current[store] = after
            codes_b[store] = after.astype(BF16)

        for yy in range(2):
            for half in range(2):
                advance(yy, half)
        if last:
            store = pltpu.make_async_copy(codes_b.at[:, :, :, own], codes_out.at[:, :, core], local_sem.at[0])
            start(copy_to(codes_b.at[:, :, :, lanes_of(1 - core)], codes_out.at[:, :, core], 2, whole_r.at[1], partner))
            store.start()

        def atoms_store(p):
            return pltpu.make_async_copy(atoms_ref.at[slab(p), :], atoms_out.at[slab(p), :], local_sem.at[2 + p])

        def summed(lay, p):
            return grad[lay, slab(p), :] + y_recv[it, lay, slab(p), :].astype(F32)

        def finish(p):
            total = keep[slab(p), :]
            for d in others:
                arrived(z_recv.at[it, layers[d], slab(p), :], gz_r.at[layers[d], p])
                total = total + z_recv[it, layers[d], slab(p), :].astype(F32)
            updated = atoms_ref[slab(p), :] + factor * total
            fresh = updated / jnp.sqrt(jnp.mean(updated * updated, axis=1, keepdims=True) + EPSILON)
            atoms_ref[slab(p), :] = fresh
            if last:
                atoms_store(p).start()
            else:
                atoms_b[it + 1, z, y, slab(p), :] = fresh.astype(BF16)
                offer(it + 1, p)

        for p in range(pieces):
            for d in order:
                arrived(y_recv.at[it, layers[d], slab(p), :], gy_r.at[d, p])
                if d == nz - 1:
                    keep[slab(p), :] = summed(layers[d], p)
                else:
                    z_send[it, layers[d], slab(p), :] = summed(layers[d], p).astype(BF16)
                    start(z_copy(layers[d], p))
                if d == nz - 2 and p:
                    finish(p - 1)
        finish(pieces - 1)

    arrived(codes_out.at[:, :, 1 - core], whole_r.at[1])
    for store in [store, residual_store] + [atoms_store(p) for p in range(pieces)]:
        store.wait()
    for copy, when in sent:
        if when is None:
            copy.wait_send()
        else:
            pl.when(when)(copy.wait_send)


def on_device(n, signal, codes, dictionary, thresholds):
    _, atom_count, time_len = codes.shape
    rows, lag_count = dictionary.shape
    nz = n // 4
    width = 2 * time_len
    pieces = pieces_of(rows)
    vmem, dma = pltpu.VMEM, pltpu.SemaphoreType.DMA
    outside = pl.BlockSpec(memory_space=pltpu.HBM)
    piece = (rows, lag_count)
    split = (nz, 2, 2, rows, time_len)
    given = [
        pltpu.with_memory_space_constraint(x, pltpu.HBM)
        for x in (signal, codes.reshape(split), dictionary, thresholds[None, :])
    ]
    made = tuple(
        pl.pallas_call(
            functools.partial(kernel, n),
            name="learn",
            out_shape=(vmem(split, BF16), vmem(piece, F32), vmem(signal.shape, F32)),
            in_specs=[outside] * 4,
            out_specs=(pl.BlockSpec(memory_space=pl.ANY),) * 3,
            scratch_shapes=[
                vmem(piece, F32),
                vmem(signal.shape, F32),
                vmem(piece, F32),
                vmem((1, atom_count), F32),
                vmem((atom_count, 1), F32),
                vmem((nz, 2, rows, 1), F32),
                vmem((nz, 2, rows, width), BF16),
                vmem((nz, 2, rows, width), F32),
                vmem((ITERS, nz, 2, *piece), BF16),
                vmem((lag_count, width), F32),
                vmem((width, lag_count), BF16),
                vmem((nz, *piece), F32),
                vmem(piece, F32),
                vmem((1, width + lag_count), F32),
                vmem((ITERS, 1, width + lag_count), F32),
                vmem((ITERS, 1, width + lag_count), F32),
                vmem((ITERS, 2, 1, lag_count), F32),
                vmem((ITERS, 2, 1, lag_count), F32),
                vmem((ITERS, nz, *piece), BF16),
                vmem((ITERS, nz, *piece), BF16),
                vmem((ITERS, nz, *piece), BF16),
                vmem((ITERS, nz, *piece), BF16),
                dma((4,)),
                dma((6,)),
                dma((2,)),
                dma((ITERS, 3)),
                dma((nz, pieces)),
                dma((1,)),
                dma((nz, pieces)),
                dma((nz, pieces)),
            ],
            compiler_params=pltpu.CompilerParams(
                collective_id=0, has_side_effects=True, vmem_limit_bytes=48_000_000
            ),
        )(*given)
    )

    def publish(codes_ref, atoms_ref, residual_ref, codes_out, atoms_out, residual_out, sems):
        pairs = [(codes_ref, codes_out), (atoms_ref, atoms_out), (residual_ref, residual_out)]
        puts = [pltpu.make_async_copy(src, dst, sems.at[i]) for i, (src, dst) in enumerate(pairs)]
        for put in puts:
            put.start()
        for put in puts:
            put.wait()

    codes_out, atoms_out, residual_out = pl.pallas_call(
        publish,
        name="publish",
        out_shape=tuple(jax.ShapeDtypeStruct(x.shape, x.dtype) for x in made),
        in_specs=[pl.BlockSpec(memory_space=pl.ANY)] * 3,
        out_specs=(outside,) * 3,
        scratch_shapes=[dma((3,))],
        compiler_params=pltpu.CompilerParams(vmem_limit_bytes=1_000_000),
    )(*made)
    return codes_out.reshape(codes.shape), atoms_out, residual_out


def solution(mesh):
    return jax.shard_map(
        functools.partial(on_device, mesh.shape["tm"]),
        mesh=mesh,
        in_specs=(P("groups", "tm"), P("groups", None, "tm"), P("tm", None), P()),
        out_specs=(P("groups", None, "tm"), P(("groups", "tm"), None), P("groups", "tm")),
        check_vma=False,
    )
```

time: 63.8 us -> 56.9 us (0.89)
  Pallas kernels: 63.1 us -> 56.1 us
    pallas_call x1, Pallas kernels: 61 us -> 55 us  [on_device(): pl.pallas_call(functools.partial(kernel, n), name='learn', out_shape=(vme...]
    pallas_call x1, Pallas kernels: 2.06 us -> 1.03 us  [on_device(): pl.pallas_call(publish, name='publish', out_shape=tuple((jax.ShapeDtypeSt...]
where the time goes in v1:
time: 56.9 us; the launch traced here: 56.7 us
  Pallas kernels  56.1 us (99%)
  between operations  0.64 us (1%)
    pallas_call x1, Pallas kernels, on_device(): pl.pallas_call(functools.partial(kernel, n), name='learn', out_shape=(vme...  55 us

profile of v1, /device:TPU:0, one launch (start us, length us, event | category | flops | bytes accessed | tf_op | source)
XLA Modules:
  0.0 56.7 jit_solution(13767061140677067741)
XLA Ops:
  0.6 55.0 %learn.1 = (bf16[4,2,2,64,512]{4,3,2,1,0:T(8,128)(2,1)S(1)}, f32[64,512]{1,0:T(8,128)S(1)}, f32[1,512]{1,0:T(1,128)S(1)}) custom-call(f32[1,512]{1,0:T(1,128)} %signal_hbm.1, bf16[4,2,2,64,512]{4,3,2,1,0:T(8,128)(2,1)} %bitcast.3, f32[64,512]{1,0:T(8,128)} %dictionary_hbm.1, f32[1,1024]{1,0:T(1,128)} %bitcast.4), custom_call_target="tpu_custom_call" | custom-call | tf_op jit(solution)/shard_map/learn/pallas_call | solution.py:350
  55.7 1.0 %publish.1 = (bf16[4,2,2,64,512]{4,3,2,1,0:T(8,128)(2,1)}, f32[64,512]{1,0:T(8,128)}, f32[1,512]{1,0:T(1,128)}) custom-call(bf16[4,2,2,64,512]{4,3,2,1,0:T(8,128)(2,1)S(1)} %get-tuple-element.9.codes_ref, f32[64,512]{1,0:T(8,128)S(1)} %get-tuple-element.10.atoms_ref, f32[1,512]{1,0:T(1,128)S(1)} %get-tuple-element.11.residual_ref), custom_call_target="tpu_custom_call" | custom-call | tf_op jit(solution)/shard_map/publish/pallas_call | solution.py:402

commit v2 on v1

v2 whole, which is shorter than its diff:
```python
import functools

import jax
import jax.numpy as jnp
from jax import lax
from jax.experimental import pallas as pl
from jax.experimental.pallas import tpu as pltpu
from jax.sharding import PartitionSpec as P

ITERS = 2
CODE_STEP = 6.0
EPSILON = 1e-06
LANES = 128
MESH = pl.DeviceIdType.MESH
BF16, F32 = jnp.bfloat16, jnp.float32
PIECES = 2


def pieces_of(rows):
    return max(1, min(PIECES, rows // 16))


def rolled(x, shift):
    width = x.shape[1]
    shift = shift % width
    return x if shift == 0 else pltpu.roll(x, shift, 1)


def skew_total(lagged):
    lag_count, time_len = lagged.shape
    width = lag_count + time_len
    total = None
    for a in range(LANES // 8):
        part = None
        for b in range(lag_count // LANES):
            block = lagged[pl.ds(b * LANES + a * 8, 8), :]
            pieces = [block]
            if b:
                pieces.insert(0, jnp.zeros((8, b * LANES), F32))
            if width - b * LANES - time_len:
                pieces.append(jnp.zeros((8, width - b * LANES - time_len), F32))
            block = jnp.concatenate(pieces, axis=1)
            part = block if part is None else part + block
        part = rolled(part, 8 * a)
        total = part if total is None else total + part
    for step in (4, 2, 1):
        total = total + pltpu.roll(rolled(total, step), 8 - step, 0)
    return total[0:1, :]


def fill_frames(frames, extended):
    lag_count, length = frames.shape
    width = extended.shape[1]
    base = jnp.broadcast_to(extended, (8, width))
    row = lax.broadcasted_iota(jnp.int32, (8, width), 0)
    for step in (1, 2, 4):
        base = jnp.where((row // step) % 2 == 1, rolled(base, width - step), base)
    for a in range(LANES // 16):
        low, high = rolled(base, width - 16 * a), rolled(base, width - 16 * a - 8)
        both = jnp.concatenate([low, high], axis=0).astype(BF16)
        for b in range(lag_count // LANES):
            frames[pl.ds(b * LANES + a * 16, 16), :] = both[:, b * LANES : b * LANES + length]


def kernel(
    n, signal_hbm, codes_hbm, dictionary_hbm, thresholds_hbm,
    codes_out, atoms_out, residual_out,
    atoms_ref, rest, signal_ref, thresholds_ref, cutoffs_all, cutoffs, codes_b, current, atoms_b, codes_main, lagged,
    frames, grad, extended_ref, shares, from_previous, from_following,
    sum_send, sum_recv, last_recv,
    local_sem, send_sem, codes_r, halo_r, line_r, sum_r, full_r, out_r,
):
    rows, lag_count = dictionary_hbm.shape
    _, lines, _, length = codes_main.shape
    team = 8
    half = lag_count // 2
    width = length - half
    atom_count = lines * team * rows
    factor = (atom_count * lag_count) ** (-0.5)
    slab_len = width // 4
    pieces = pieces_of(rows)
    part = rows // pieces
    me = lax.axis_index("tm")
    pos, group = me % team, me // team
    core, chip = pos % 2, pos // 2

    def flipped(bits):
        at = 0
        for bit in (4, 2, 1):
            one = (pos // bit) % 2
            at = at + bit * ((1 - one) if bits & bit else one)
        return at

    def member(at, group_of=group):
        return group_of * team + at

    partner = member(flipped(1))
    mates = [(group + k) % lines for k in range(1, lines)]

    def copy_to(src, dst, send, recv_sem, target):
        return pltpu.make_async_remote_copy(
            src_ref=src, dst_ref=dst, send_sem=send_sem.at[send], recv_sem=recv_sem,
            device_id={"tm": target}, device_id_type=MESH,
        )

    def arrived(ref, recv_sem):
        pltpu.make_async_copy(ref, ref, recv_sem).wait()

    sent = []

    def start(copy, when=None):
        if when is None:
            copy.start()
        else:
            pl.when(when)(copy.start)
        sent.append((copy, when))

    def lanes_of(at):
        return pl.ds(pl.multiple_of(at * lag_count, LANES), lag_count)

    def slab(p):
        return pl.ds(p * part, part)

    loads = [
        pltpu.make_async_copy(dictionary_hbm, atoms_ref.at[group], local_sem.at[0]),
        pltpu.make_async_copy(signal_hbm, signal_ref, local_sem.at[1]),
        pltpu.make_async_copy(thresholds_hbm, thresholds_ref, local_sem.at[2]),
        pltpu.make_async_copy(codes_hbm.at[:, chip, core], codes_main.at[0, :, :, lanes_of(pos)], codes_r.at[0]),
        pltpu.make_async_copy(codes_hbm.at[:, :, core], codes_b.at[:, :, :, lanes_of(core)], codes_r.at[1]),
    ]
    for load in loads:
        load.start()

    barrier = pltpu.get_barrier_semaphore()

    def greet(target):
        pl.semaphore_signal(barrier, inc=1, device_id={"tm": target}, device_id_type=MESH)

    for bits in range(1, team):
        greet(member(flipped(bits)))
    for mate in mates:
        greet(member(pos, mate))

    loads[0].wait()
    atoms_b[0, group, chip] = atoms_ref[group].astype(BF16)
    rest[group] = (atoms_ref[group] - atoms_b[0, group, chip].astype(F32)).astype(BF16)
    pl.semaphore_wait(barrier, team - 1 + lines - 1)

    for mate in mates:
        held = atoms_b.at[0, group, chip]
        start(copy_to(held, held, 0, line_r.at[0], member(pos, mate)))
    for bits in (7, 6, 3, 2, 5, 4, 1):
        at = flipped(bits)
        start(
            copy_to(
                codes_hbm.at[:, at // 2, at % 2], codes_main.at[0, :, :, lanes_of(pos)], 1, codes_r.at[0], member(at)
            )
        )
    start(copy_to(codes_hbm.at[:, :, 1 - core], codes_b.at[:, :, :, lanes_of(core)], 1, codes_r.at[1], partner))
    codes_main[0, :, :, pl.ds(width, half)] = jnp.zeros((lines, rows, half), BF16)
    codes_main[1, :, :, pl.ds(0, half)] = jnp.zeros((lines, rows, half), BF16)
    loads[2].wait()
    cutoffs_all[...] = CODE_STEP * jnp.broadcast_to(thresholds_ref[...], (8, atom_count)).T[:, 0:1]
    for i in range(lines):
        for u in range(team // 2):
            at = pl.multiple_of((i * team + 2 * u + core) * rows, rows)
            cutoffs[i, u] = cutoffs_all[pl.ds(at, rows), :]
    loads[1].wait()

    def share_atoms(it, p):
        held = atoms_b.at[it, :, chip, slab(p), :]
        for bits in (6, 2, 4):
            start(copy_to(held, held, 0, full_r.at[it], member(flipped(bits))))

    def shrunk(before, matched, cutoff):
        shrink = before + (CODE_STEP * factor) * matched
        return shrink - jnp.minimum(jnp.maximum(shrink, -cutoff), cutoff)

    def product(atoms, at):
        low = jnp.dot(atoms[:, :half], frames[:, pl.ds(at, lag_count)], preferred_element_type=F32)
        return low + jnp.dot(atoms[:, half:], frames[:, pl.ds(at + half, lag_count)], preferred_element_type=F32)

    def advance(it, side):
        at = pl.multiple_of((2 * chip + side) * lag_count, LANES)
        for i in range(lines):
            matched = product(atoms_b[it, i].reshape(4 * rows, lag_count), at)
            store = (i, slice(None), slice(None), lanes_of(side))
            before = codes_b[store].astype(F32) if it == 0 else current[store]
            after = shrunk(before, matched.reshape(4, rows, lag_count), cutoffs[i])
            if it < ITERS - 1:
                current[store] = after
            codes_b[store] = after.astype(BF16)

    def advance_main(it):
        atoms = atoms_b[it, :, chip].reshape(lines * rows, lag_count)
        cutoff = cutoffs[:, chip]
        for i in range(team):
            store = (slice(None), slice(None), pl.ds(i * lag_count, lag_count))
            matched = product(atoms, i * lag_count).reshape(lines, rows, lag_count)
            if it == 0:
                before = codes_main[(0, *store)].astype(F32)
            after = shrunk(before, matched, cutoff).astype(BF16)
            codes_main[(0, *store)] = after
            codes_main[1, :, :, pl.ds(i * lag_count + half, lag_count)] = after

    early = pieces // 2

    for it in range(ITERS):
        last = it == ITERS - 1
        if it == 0:
            arrived(atoms_b.at[0, pl.ds(0, lines - 1), 0], line_r.at[0])
            arrived(codes_main.at[0, :, :, pl.ds(0, width)], codes_r.at[0])
            for mate in mates:
                start(copy_to(rest.at[group], rest.at[group], 0, line_r.at[1], member(pos, mate)))
            codes_main[1, :, :, pl.ds(half, width)] = codes_main[0, :, :, pl.ds(0, width)]
        atoms = atoms_b[it, :, chip].reshape(lines * rows, lag_count)
        lagged[...] = lax.dot_general(
            jnp.concatenate([atoms[:, :half], atoms[:, half:]], axis=0),
            codes_main[...].reshape(2 * lines * rows, length),
            (((0,), (0,)), ((), ())), preferred_element_type=F32,
        )
        shares[it, pos] = -factor * skew_total(lagged)
        shares[it, pos, :, lanes_of(pos)] += signal_ref[...]

        for bits in (7, 6, 3, 2, 5, 4, 1):
            held = shares.at[it, pos]
            start(copy_to(held, held, 2, halo_r.at[it, 0], member(flipped(bits))))
        for at in range(team):
            start(
                copy_to(
                    shares.at[it, pos, :, pl.ds(width, lag_count)], from_previous.at[it, pos],
                    2, halo_r.at[it, 1], member(at, group + 1),
                ),
                group < lines - 1,
            )
            start(
                copy_to(
                    shares.at[it, pos, :, pl.ds(0, lag_count)], from_following.at[it, pos],
                    2, halo_r.at[it, 2], member(at, group - 1),
                ),
                group > 0,
            )

        @pl.when(group == 0)
        def _():
            from_previous[it] = jnp.zeros_like(from_previous[it])

        @pl.when(group == lines - 1)
        def _():
            from_following[it] = jnp.zeros_like(from_following[it])

        if it == 1:
            arrived(atoms_b.at[0, :, pl.ds(0, 3)], full_r.at[0])
            arrived(codes_b, codes_r.at[1])
            for side in range(2):
                advance(0, side)

        arrived(shares.at[it, pl.ds(0, team - 1)], halo_r.at[it, 0])
        pl.when(group > 0)(functools.partial(arrived, from_previous.at[it], halo_r.at[it, 1]))
        pl.when(group < lines - 1)(functools.partial(arrived, from_following.at[it], halo_r.at[it, 2]))
        for p in range(early, pieces) if it else ():
            share_atoms(it, p)

        total, head, tail = shares[it, 0], from_previous[it, 0], from_following[it, 0]
        for at in range(1, team):
            total, head, tail = total + shares[it, at], head + from_previous[it, at], tail + from_following[it, at]
        residual = jnp.concatenate(
            [total[:, :lag_count] + head, total[:, lag_count:width], total[:, width:] + tail], axis=1
        )
        lane = lax.broadcasted_iota(jnp.int32, residual.shape, 1)
        known = width + lag_count * jnp.minimum(lines - 1 - group, 1)
        residual = jnp.where(lane < known, residual, 0.0)
        if last:
            extended_ref[...] = residual
            residual_store = pltpu.make_async_copy(extended_ref.at[:, lanes_of(pos)], residual_out, local_sem.at[1])
            residual_store.start()
        fill_frames(frames, residual.astype(BF16).astype(F32))

        for side in range(2):
            total = None
            for i in range(width // half):
                codes = codes_main[0, :, :, pl.ds(i * half, half)].reshape(lines * rows, half)
                term = jnp.dot(codes, frames[:, pl.ds((i + side) * half, half)], preferred_element_type=F32)
                total = term if total is None else total + term
            grad[:, :, pl.ds(side * half, half)] = total.reshape(lines, rows, half)
            sum_send[it, side] = total.reshape(lines, rows, half).astype(BF16)
            for mate in mates:
                if not last:
                    start(copy_to(sum_send.at[it, side], sum_recv.at[group, side], 3, sum_r.at[0], member(pos, mate)))
                else:
                    start(
                        copy_to(sum_send.at[it, side, mate], last_recv.at[group, side], 3, sum_r.at[1], member(pos, mate))
                    )

        if not last:
            for p in range(pieces) if it == 0 else ():
                share_atoms(0, p)
            advance_main(it)
            arrived(rest.at[pl.ds(0, lines - 1)], line_r.at[1])
            for mate in mates:
                atoms_ref[mate] = atoms_b[0, mate, chip].astype(F32) + rest[mate].astype(F32)
            arrived(sum_recv.at[pl.ds(0, lines - 1)], sum_r.at[0])
            total = grad[...]
            for mate in mates:
                theirs = jnp.concatenate([sum_recv[mate, 0], sum_recv[mate, 1]], axis=2)
                total = total + theirs.astype(F32)
            updated = atoms_ref[...] + factor * total
            fresh = updated / jnp.sqrt(jnp.mean(updated * updated, axis=2, keepdims=True) + EPSILON)
            atoms_ref[...] = fresh
            atoms_b[it + 1, :, chip] = fresh.astype(BF16)
            for p in range(early):
                share_atoms(it + 1, p)
            continue

        arrived(atoms_b.at[it, :, pl.ds(0, 3)], full_r.at[it])
        advance(it, 1 - core)
        start(copy_to(codes_b.at[:, :, :, lanes_of(1 - core)], codes_out.at[:, :, core], 1, out_r.at[0], partner))
        advance(it, core)
        store = pltpu.make_async_copy(codes_b.at[:, :, :, lanes_of(core)], codes_out.at[:, :, core], local_sem.at[0])
        store.start()
        arrived(last_recv.at[pl.ds(0, lines - 1)], sum_r.at[1])
        total = grad[group]
        for mate in mates:
            total = total + jnp.concatenate([last_recv[mate, 0], last_recv[mate, 1]], axis=1).astype(F32)
        updated = atoms_ref[group] + factor * total
        atoms_ref[group] = updated / jnp.sqrt(jnp.mean(updated * updated, axis=1, keepdims=True) + EPSILON)
        atoms_store = pltpu.make_async_copy(atoms_ref.at[group], atoms_out, local_sem.at[2])
        atoms_store.start()

    arrived(codes_out.at[:, :, 1 - core], out_r.at[0])
    for put in (store, residual_store, atoms_store):
        put.wait()
    for copy, when in sent:
        if when is None:
            copy.wait_send()
        else:
            pl.when(when)(copy.wait_send)


def on_device(n, signal, codes, dictionary, thresholds):
    _, atom_count, time_len = codes.shape
    rows, lag_count = dictionary.shape
    lines, team = n // 8, 8
    width, half = team * time_len, lag_count // 2
    vmem, dma = pltpu.VMEM, pltpu.SemaphoreType.DMA
    outside = pl.BlockSpec(memory_space=pltpu.HBM)
    piece = (rows, lag_count)
    split = (lines, 4, 2, rows, time_len)
    given = [
        pltpu.with_memory_space_constraint(x, pltpu.HBM)
        for x in (signal, codes.reshape(split), dictionary, thresholds[None, :])
    ]
    made = tuple(
        pl.pallas_call(
            functools.partial(kernel, n),
            name="learn",
            out_shape=(vmem(split, BF16), vmem(piece, F32), vmem(signal.shape, F32)),
            in_specs=[outside] * 4,
            out_specs=(pl.BlockSpec(memory_space=pl.ANY),) * 3,
            scratch_shapes=[
                vmem((lines, *piece), F32),
                vmem((lines, *piece), BF16),
                vmem(signal.shape, F32),
                vmem((1, atom_count), F32),
                vmem((atom_count, 1), F32),
                vmem((lines, 4, rows, 1), F32),
                vmem((lines, 4, rows, 2 * time_len), BF16),
                vmem((lines, 4, rows, 2 * time_len), F32),
                vmem((ITERS, lines, 4, *piece), BF16),
                vmem((2, lines, rows, width + half), BF16),
                vmem((half, width + half), F32),
                vmem((half, width + half), BF16),
                vmem((lines, *piece), F32),
                vmem((1, width + lag_count), F32),
                vmem((ITERS, team, 1, width + lag_count), F32),
                vmem((ITERS, team, 1, lag_count), F32),
                vmem((ITERS, team, 1, lag_count), F32),
                vmem((ITERS, 2, lines, rows, half), BF16),
                vmem((lines, 2, lines, rows, half), BF16),
                vmem((lines, 2, rows, half), BF16),
                dma((3,)),
                dma((4,)),
                dma((2,)),
                dma((ITERS, 3)),
                dma((2,)),
                dma((2,)),
                dma((ITERS,)),
                dma((1,)),
            ],
            compiler_params=pltpu.CompilerParams(
                collective_id=0, has_side_effects=True, vmem_limit_bytes=48_000_000
            ),
        )(*given)
    )

    def publish(codes_ref, atoms_ref, residual_ref, codes_out, atoms_out, residual_out, sems):
        pairs = [(codes_ref, codes_out), (atoms_ref, atoms_out), (residual_ref, residual_out)]
        puts = [pltpu.make_async_copy(src, dst, sems.at[i]) for i, (src, dst) in enumerate(pairs)]
        for put in puts:
            put.start()
        for put in puts:
            put.wait()

    codes_out, atoms_out, residual_out = pl.pallas_call(
        publish,
        name="publish",
        out_shape=tuple(jax.ShapeDtypeStruct(x.shape, x.dtype) for x in made),
        in_specs=[pl.BlockSpec(memory_space=pl.ANY)] * 3,
        out_specs=(outside,) * 3,
        scratch_shapes=[dma((3,))],
        compiler_params=pltpu.CompilerParams(vmem_limit_bytes=1_000_000),
    )(*made)
    return codes_out.reshape(codes.shape), atoms_out, residual_out


def solution(mesh):
    return jax.shard_map(
        functools.partial(on_device, mesh.shape["tm"]),
        mesh=mesh,
        in_specs=(P("groups", "tm"), P("groups", None, "tm"), P("tm", None), P()),
        out_specs=(P("groups", None, "tm"), P(("groups", "tm"), None), P("groups", "tm")),
        check_vma=False,
    )
```

time: 56.9 us -> 52.7 us (0.926)
  Pallas kernels: 56.1 us -> 51.9 us
    pallas_call x1, Pallas kernels: 55 us -> 50.8 us  [on_device(): pl.pallas_call(functools.partial(kernel, n), name='learn', out_shape=(vme...]
where the time goes in v2:
time: 52.7 us; the launch traced here: 52.5 us
  Pallas kernels  51.9 us (98%)
  between operations  0.64 us (1%)
    pallas_call x1, Pallas kernels, on_device(): pl.pallas_call(functools.partial(kernel, n), name='learn', out_shape=(vme...  50.8 us

profile of v2, /device:TPU:0, one launch (start us, length us, event | category | flops | bytes accessed | tf_op | source)
XLA Modules:
  0.0 52.5 jit_solution(11826098158801177592)
XLA Ops:
  0.6 50.8 %learn.1 = (bf16[2,4,2,64,512]{4,3,2,1,0:T(8,128)(2,1)S(1)}, f32[64,512]{1,0:T(8,128)S(1)}, f32[1,512]{1,0:T(1,128)S(1)}) custom-call(f32[1,512]{1,0:T(1,128)} %signal_hbm.1, bf16[2,4,2,64,512]{4,3,2,1,0:T(8,128)(2,1)} %bitcast.3, f32[64,512]{1,0:T(8,128)} %dictionary_hbm.1, f32[1,1024]{1,0:T(1,128)} %bitcast.4), custom_call_target="tpu_custom_call" | custom-call | tf_op jit(solution)/shard_map/learn/pallas_call | solution.py:354
  51.5 1.0 %publish.1 = (bf16[2,4,2,64,512]{4,3,2,1,0:T(8,128)(2,1)}, f32[64,512]{1,0:T(8,128)}, f32[1,512]{1,0:T(1,128)}) custom-call(bf16[2,4,2,64,512]{4,3,2,1,0:T(8,128)(2,1)S(1)} %get-tuple-element.9.codes_ref, f32[64,512]{1,0:T(8,128)S(1)} %get-tuple-element.10.atoms_ref, f32[1,512]{1,0:T(1,128)S(1)} %get-tuple-element.11.residual_ref), custom_call_target="tpu_custom_call" | custom-call | tf_op jit(solution)/shard_map/publish/pallas_call | solution.py:404

commit v3 on v2

--- a/solution.py
+++ b/solution.py
@@ -13,7 +13,7 @@
 LANES = 128
 MESH = pl.DeviceIdType.MESH
 BF16, F32 = jnp.bfloat16, jnp.float32
-PIECES = 2
+PIECES = 1
 
 
 def pieces_of(rows):
@@ -26,40 +26,44 @@
     return x if shift == 0 else pltpu.roll(x, shift, 1)
 
 
-def skew_total(lagged):
-    lag_count, time_len = lagged.shape
-    width = lag_count + time_len
+def lanes_from(ref, row, start, width):
+    length = ref.shape[1]
+    low, high = max(start, 0), min(start + width, length)
+    if low >= high:
+        return jnp.zeros((8, width), F32)
+    pieces = [ref[pl.ds(row, 8), pl.ds(low, high - low)]]
+    if low > start:
+        pieces.insert(0, jnp.zeros((8, low - start), F32))
+    if start + width > high:
+        pieces.append(jnp.zeros((8, start + width - high), F32))
+    return pieces[0] if len(pieces) == 1 else jnp.concatenate(pieces, axis=1)
+
+
+def skew_total(lagged, start, length):
     total = None
     for a in range(LANES // 8):
         part = None
-        for b in range(lag_count // LANES):
-            block = lagged[pl.ds(b * LANES + a * 8, 8), :]
-            pieces = [block]
-            if b:
-                pieces.insert(0, jnp.zeros((8, b * LANES), F32))
-            if width - b * LANES - time_len:
-                pieces.append(jnp.zeros((8, width - b * LANES - time_len), F32))
-            block = jnp.concatenate(pieces, axis=1)
+        for b in range(lagged.shape[0] // LANES):
+            block = lanes_from(lagged, b * LANES + a * 8, start - LANES - b * LANES, length + LANES)
             part = block if part is None else part + block
         part = rolled(part, 8 * a)
         total = part if total is None else total + part
     for step in (4, 2, 1):
         total = total + pltpu.roll(rolled(total, step), 8 - step, 0)
-    return total[0:1, :]
-
-
-def fill_frames(frames, extended):
-    lag_count, length = frames.shape
-    width = extended.shape[1]
-    base = jnp.broadcast_to(extended, (8, width))
+    return total[0:1, LANES:]
+
+
+def fill_frames(frames, extended, start, length):
+    width = length + 2 * LANES
+    base = jnp.broadcast_to(extended[:, start : start + width], (8, width))
     row = lax.broadcasted_iota(jnp.int32, (8, width), 0)
     for step in (1, 2, 4):
         base = jnp.where((row // step) % 2 == 1, rolled(base, width - step), base)
     for a in range(LANES // 16):
         low, high = rolled(base, width - 16 * a), rolled(base, width - 16 * a - 8)
         both = jnp.concatenate([low, high], axis=0).astype(BF16)
-        for b in range(lag_count // LANES):
-            frames[pl.ds(b * LANES + a * 16, 16), :] = both[:, b * LANES : b * LANES + length]
+        for b in range(frames.shape[0] // LANES):
+            frames[pl.ds(b * LANES + a * 16, 16), pl.ds(start, length)] = both[:, b * LANES : b * LANES + length]
 
 
 def kernel(
@@ -166,11 +170,13 @@
             at = pl.multiple_of((i * team + 2 * u + core) * rows, rows)
             cutoffs[i, u] = cutoffs_all[pl.ds(at, rows), :]
     loads[1].wait()
+    extended_ref[0] = jnp.zeros((1, width + lag_count), F32)
+    extended_ref[0, :, lanes_of(pos)] = signal_ref[...]
 
     def share_atoms(it, p):
         held = atoms_b.at[it, :, chip, slab(p), :]
-        for bits in (6, 2, 4):
-            start(copy_to(held, held, 0, full_r.at[it], member(flipped(bits))))
+        for bits in (4, 6, 2):
+            start(copy_to(held, held, 0, full_r.at[it, bits // 2 - 1], member(flipped(bits))))
 
     def shrunk(before, matched, cutoff):
         shrink = before + (CODE_STEP * factor) * matched
@@ -180,16 +186,18 @@
         low = jnp.dot(atoms[:, :half], frames[:, pl.ds(at, lag_count)], preferred_element_type=F32)
         return low + jnp.dot(atoms[:, half:], frames[:, pl.ds(at + half, lag_count)], preferred_element_type=F32)
 
-    def advance(it, side):
+    def advance(it, side, rows_of, count):
         at = pl.multiple_of((2 * chip + side) * lag_count, LANES)
-        for i in range(lines):
-            matched = product(atoms_b[it, i].reshape(4 * rows, lag_count), at)
-            store = (i, slice(None), slice(None), lanes_of(side))
-            before = codes_b[store].astype(F32) if it == 0 else current[store]
-            after = shrunk(before, matched.reshape(4, rows, lag_count), cutoffs[i])
-            if it < ITERS - 1:
-                current[store] = after
-            codes_b[store] = after.astype(BF16)
+        matched = product(atoms_b[(it, *rows_of)].reshape(count * rows, lag_count), at)
+        store = (*rows_of, slice(None), lanes_of(side))
+        before = codes_b[store].astype(F32) if it == 0 else current[store]
+        after = shrunk(before, matched.reshape(count, rows, lag_count), cutoffs[rows_of])
+        if it < ITERS - 1:
+            current[store] = after
+        codes_b[store] = after.astype(BF16)
+
+    def wait_full(it, bits):
+        arrived(atoms_b.at[it, :, flipped(bits) // 2], full_r.at[it, bits // 2 - 1])
 
     def advance_main(it):
         atoms = atoms_b[it, :, chip].reshape(lines * rows, lag_count)
@@ -203,7 +211,8 @@
             codes_main[(0, *store)] = after
             codes_main[1, :, :, pl.ds(i * lag_count + half, lag_count)] = after
 
-    early = pieces // 2
+    early = 0
+    whole, chunk = width + lag_count, 5 * half
 
     for it in range(ITERS):
         last = it == ITERS - 1
@@ -214,32 +223,45 @@
                 start(copy_to(rest.at[group], rest.at[group], 0, line_r.at[1], member(pos, mate)))
             codes_main[1, :, :, pl.ds(half, width)] = codes_main[0, :, :, pl.ds(0, width)]
         atoms = atoms_b[it, :, chip].reshape(lines * rows, lag_count)
-        lagged[...] = lax.dot_general(
-            jnp.concatenate([atoms[:, :half], atoms[:, half:]], axis=0),
-            codes_main[...].reshape(2 * lines * rows, length),
-            (((0,), (0,)), ((), ())), preferred_element_type=F32,
-        )
-        shares[it, pos] = -factor * skew_total(lagged)
-        shares[it, pos, :, lanes_of(pos)] += signal_ref[...]
-
-        for bits in (7, 6, 3, 2, 5, 4, 1):
-            held = shares.at[it, pos]
-            start(copy_to(held, held, 2, halo_r.at[it, 0], member(flipped(bits))))
-        for at in range(team):
+        pair = jnp.concatenate([atoms[:, :half], atoms[:, half:]], axis=0)
+
+        def correlate(at):
+            picked = pl.ds(at, min(chunk, length - at))
+            lagged[:, picked] = lax.dot_general(
+                pair, codes_main[:, :, :, picked].reshape(2 * lines * rows, picked.size),
+                (((0,), (0,)), ((), ())), preferred_element_type=F32,
+            )
+
+        correlate(0)
+        for at in range(0, whole, chunk):
+            if at + chunk < length:
+                correlate(at + chunk)
+            span = pl.ds(at, min(chunk, whole - at))
+            shares[it, pos, :, span] = extended_ref[0, :, span] - factor * skew_total(lagged, at, span.size)
+            if at // chunk % 2 == 0:
+                continue
+            held = shares.at[it, pos, :, pl.ds(at - chunk, chunk + span.size)]
+            for bits in (7, 6, 3, 2, 5, 4, 1):
+                start(copy_to(held, held, 2, halo_r.at[it, 0], member(flipped(bits))))
+            if at == chunk:
+                for to in range(team):
+                    start(
+                        copy_to(
+                            shares.at[it, pos, :, pl.ds(0, lag_count)], from_following.at[it, pos],
+                            2, halo_r.at[it, 2], member(to, group - 1),
+                        ),
+                        group > 0,
+                    )
+        for to in range(team):
             start(
                 copy_to(
                     shares.at[it, pos, :, pl.ds(width, lag_count)], from_previous.at[it, pos],
-                    2, halo_r.at[it, 1], member(at, group + 1),
+                    2, halo_r.at[it, 1], member(to, group + 1),
                 ),
                 group < lines - 1,
             )
-            start(
-                copy_to(
-                    shares.at[it, pos, :, pl.ds(0, lag_count)], from_following.at[it, pos],
-                    2, halo_r.at[it, 2], member(at, group - 1),
-                ),
-                group > 0,
-            )
+        for p in range(early, pieces) if it else ():
+            share_atoms(it, p)
 
         @pl.when(group == 0)
         def _():
@@ -250,17 +272,16 @@
             from_following[it] = jnp.zeros_like(from_following[it])
 
         if it == 1:
-            arrived(atoms_b.at[0, :, pl.ds(0, 3)], full_r.at[0])
+            for bits in (6, 2, 4):
+                wait_full(0, bits)
             arrived(codes_b, codes_r.at[1])
-            for side in range(2):
-                advance(0, side)
+            for i in range(lines):
+                for side in range(2):
+                    advance(0, side, (i, slice(None)), team // 2)
 
         arrived(shares.at[it, pl.ds(0, team - 1)], halo_r.at[it, 0])
         pl.when(group > 0)(functools.partial(arrived, from_previous.at[it], halo_r.at[it, 1]))
         pl.when(group < lines - 1)(functools.partial(arrived, from_following.at[it], halo_r.at[it, 2]))
-        for p in range(early, pieces) if it else ():
-            share_atoms(it, p)
-
         total, head, tail = shares[it, 0], from_previous[it, 0], from_following[it, 0]
         for at in range(1, team):
             total, head, tail = total + shares[it, at], head + from_previous[it, at], tail + from_following[it, at]
@@ -271,17 +292,20 @@
         known = width + lag_count * jnp.minimum(lines - 1 - group, 1)
         residual = jnp.where(lane < known, residual, 0.0)
         if last:
-            extended_ref[...] = residual
-            residual_store = pltpu.make_async_copy(extended_ref.at[:, lanes_of(pos)], residual_out, local_sem.at[1])
+            extended_ref[1] = residual
+            residual_store = pltpu.make_async_copy(extended_ref.at[1, :, lanes_of(pos)], residual_out, local_sem.at[1])
             residual_store.start()
-        fill_frames(frames, residual.astype(BF16).astype(F32))
+        residual = residual.astype(BF16).astype(F32)
+        fill_frames(frames, residual, 0, length)
+
+        def term(i, side):
+            codes = codes_main[0, :, :, pl.ds(i * half, half)].reshape(lines * rows, half)
+            return jnp.dot(codes, frames[:, pl.ds((i + side) * half, half)], preferred_element_type=F32)
 
         for side in range(2):
             total = None
             for i in range(width // half):
-                codes = codes_main[0, :, :, pl.ds(i * half, half)].reshape(lines * rows, half)
-                term = jnp.dot(codes, frames[:, pl.ds((i + side) * half, half)], preferred_element_type=F32)
-                total = term if total is None else total + term
+                total = term(i, side) if total is None else total + term(i, side)
             grad[:, :, pl.ds(side * half, half)] = total.reshape(lines, rows, half)
             sum_send[it, side] = total.reshape(lines, rows, half).astype(BF16)
             for mate in mates:
@@ -312,12 +336,16 @@
                 share_atoms(it + 1, p)
             continue
 
-        arrived(atoms_b.at[it, :, pl.ds(0, 3)], full_r.at[it])
-        advance(it, 1 - core)
-        start(copy_to(codes_b.at[:, :, :, lanes_of(1 - core)], codes_out.at[:, :, core], 1, out_r.at[0], partner))
-        advance(it, core)
-        store = pltpu.make_async_copy(codes_b.at[:, :, :, lanes_of(core)], codes_out.at[:, :, core], local_sem.at[0])
-        store.start()
+        for bits in (0, 2, 4, 6):
+            at = flipped(bits) // 2
+            if bits:
+                wait_full(it, bits)
+            advance(it, 1 - core, (slice(None), at), lines)
+            give = codes_b.at[:, at, :, lanes_of(1 - core)]
+            start(copy_to(give, codes_out.at[:, at, core], 1, out_r.at[0], partner))
+            advance(it, core, (slice(None), at), lines)
+            keep = codes_b.at[:, at, :, lanes_of(core)]
+            pltpu.make_async_copy(keep, codes_out.at[:, at, core], local_sem.at[0]).start()
         arrived(last_recv.at[pl.ds(0, lines - 1)], sum_r.at[1])
         total = grad[group]
         for mate in mates:
@@ -328,7 +356,8 @@
         atoms_store.start()
 
     arrived(codes_out.at[:, :, 1 - core], out_r.at[0])
-    for put in (store, residual_store, atoms_store):
+    arrived(codes_out.at[:, :, core], local_sem.at[0])
+    for put in (residual_store, atoms_store):
         put.wait()
     for copy, when in sent:
         if when is None:
@@ -371,7 +400,7 @@
                 vmem((half, width + half), F32),
                 vmem((half, width + half), BF16),
                 vmem((lines, *piece), F32),
-                vmem((1, width + lag_count), F32),
+                vmem((2, 1, width + lag_count), F32),
                 vmem((ITERS, team, 1, width + lag_count), F32),
                 vmem((ITERS, team, 1, lag_count), F32),
                 vmem((ITERS, team, 1, lag_count), F32),
@@ -384,7 +413,7 @@
                 dma((ITERS, 3)),
                 dma((2,)),
                 dma((2,)),
-                dma((ITERS,)),
+                dma((ITERS, 3)),
                 dma((1,)),
             ],
             compiler_params=pltpu.CompilerParams(
@@ -394,7 +423,8 @@
     )
 
     def publish(codes_ref, atoms_ref, residual_ref, codes_out, atoms_out, residual_out, sems):
-        pairs = [(codes_ref, codes_out), (atoms_ref, atoms_out), (residual_ref, residual_out)]
+        pairs = [(codes_ref.at[:, i], codes_out.at[:, i]) for i in range(codes_ref.shape[1])]
+        pairs += [(atoms_ref, atoms_out), (residual_ref, residual_out)]
         puts = [pltpu.make_async_copy(src, dst, sems.at[i]) for i, (src, dst) in enumerate(pairs)]
         for put in puts:
             put.start()
@@ -407,7 +437,7 @@
         out_shape=tuple(jax.ShapeDtypeStruct(x.shape, x.dtype) for x in made),
         in_specs=[pl.BlockSpec(memory_space=pl.ANY)] * 3,
         out_specs=(outside,) * 3,
-        scratch_shapes=[dma((3,))],
+        scratch_shapes=[dma((6,))],
         compiler_params=pltpu.CompilerParams(vmem_limit_bytes=1_000_000),
     )(*made)
     return codes_out.reshape(codes.shape), atoms_out, residual_out

time: 52.7 us -> 50.4 us (0.956)
  Pallas kernels: 51.9 us -> 49.6 us
    pallas_call x1, Pallas kernels: 50.8 us -> 48.6 us  [on_device(): pl.pallas_call(functools.partial(kernel, n), name='learn', out_shape=(vme...]
where the time goes in v3:
time: 50.4 us; the launch traced here: 50.3 us
  Pallas kernels  49.6 us (98%)
  between operations  0.64 us (1%)
    pallas_call x1, Pallas kernels, on_device(): pl.pallas_call(functools.partial(kernel, n), name='learn', out_shape=(vme...  48.6 us
    pallas_call x1, Pallas kernels, on_device(): pl.pallas_call(publish, name='publish', out_shape=tuple((jax.ShapeDtypeSt...  1.06 us

profile of v3, /device:TPU:0, one launch (start us, length us, event | category | flops | bytes accessed | tf_op | source)
XLA Modules:
  0.0 50.3 jit_solution(12885039998121726130)
XLA Ops:
  0.6 48.6 %learn.1 = (bf16[2,4,2,64,512]{4,3,2,1,0:T(8,128)(2,1)S(1)}, f32[64,512]{1,0:T(8,128)S(1)}, f32[1,512]{1,0:T(1,128)S(1)}) custom-call(f32[1,512]{1,0:T(1,128)} %signal_hbm.1, bf16[2,4,2,64,512]{4,3,2,1,0:T(8,128)(2,1)} %bitcast.3, f32[64,512]{1,0:T(8,128)} %dictionary_hbm.1, f32[1,1024]{1,0:T(1,128)} %bitcast.4), custom_call_target="tpu_custom_call" | custom-call | tf_op jit(solution)/shard_map/learn/pallas_call | solution.py:383
  49.2 1.1 %publish.1 = (bf16[2,4,2,64,512]{4,3,2,1,0:T(8,128)(2,1)}, f32[64,512]{1,0:T(8,128)}, f32[1,512]{1,0:T(1,128)}) custom-call(bf16[2,4,2,64,512]{4,3,2,1,0:T(8,128)(2,1)S(1)} %get-tuple-element.9.codes_ref, f32[64,512]{1,0:T(8,128)S(1)} %get-tuple-element.10.atoms_ref, f32[1,512]{1,0:T(1,128)S(1)} %get-tuple-element.11.residual_ref), custom_call_target="tpu_custom_call" | custom-call | tf_op jit(solution)/shard_map/publish/pallas_call | solution.py:434

commit v4 on v3

--- a/solution.py
+++ b/solution.py
@@ -118,6 +118,13 @@
         else:
             pl.when(when)(copy.start)
         sent.append((copy, when))
+
+    def ready(copies):
+        sent.extend((copy, None) for copy in copies)
+        return copies
+
+    def step(body):
+        pl.when(me >= 0)(body)
 
     def lanes_of(at):
         return pl.ds(pl.multiple_of(at * lag_count, LANES), lag_count)
@@ -219,8 +226,6 @@
         if it == 0:
             arrived(atoms_b.at[0, pl.ds(0, lines - 1), 0], line_r.at[0])
             arrived(codes_main.at[0, :, :, pl.ds(0, width)], codes_r.at[0])
-            for mate in mates:
-                start(copy_to(rest.at[group], rest.at[group], 0, line_r.at[1], member(pos, mate)))
             codes_main[1, :, :, pl.ds(half, width)] = codes_main[0, :, :, pl.ds(0, width)]
         atoms = atoms_b[it, :, chip].reshape(lines * rows, lag_count)
         pair = jnp.concatenate([atoms[:, :half], atoms[:, half:]], axis=0)
@@ -260,6 +265,9 @@
                 ),
                 group < lines - 1,
             )
+        if it == 0:
+            for mate in mates:
+                start(copy_to(rest.at[group], rest.at[group], 0, line_r.at[1], member(pos, mate)))
         for p in range(early, pieces) if it else ():
             share_atoms(it, p)
 
@@ -303,23 +311,31 @@
             return jnp.dot(codes, frames[:, pl.ds((i + side) * half, half)], preferred_element_type=F32)
 
         for side in range(2):
-            total = None
-            for i in range(width // half):
-                total = term(i, side) if total is None else total + term(i, side)
-            grad[:, :, pl.ds(side * half, half)] = total.reshape(lines, rows, half)
-            sum_send[it, side] = total.reshape(lines, rows, half).astype(BF16)
-            for mate in mates:
-                if not last:
-                    start(copy_to(sum_send.at[it, side], sum_recv.at[group, side], 3, sum_r.at[0], member(pos, mate)))
-                else:
-                    start(
-                        copy_to(sum_send.at[it, side, mate], last_recv.at[group, side], 3, sum_r.at[1], member(pos, mate))
-                    )
+            if not last:
+                outgoing = ready([
+                    copy_to(sum_send.at[it, side], sum_recv.at[group, side], 3, sum_r.at[0], member(pos, mate))
+                    for mate in mates
+                ])
+            else:
+                outgoing = ready([
+                    copy_to(sum_send.at[it, side, mate], last_recv.at[group, side], 3, sum_r.at[1], member(pos, mate))
+                    for mate in mates
+                ])
+
+            @step
+            def _():
+                total = None
+                for i in range(width // half):
+                    total = term(i, side) if total is None else total + term(i, side)
+                grad[:, :, pl.ds(side * half, half)] = total.reshape(lines, rows, half)
+                sum_send[it, side] = total.reshape(lines, rows, half).astype(BF16)
+                for copy in outgoing:
+                    copy.start()
 
         if not last:
             for p in range(pieces) if it == 0 else ():
                 share_atoms(0, p)
-            advance_main(it)
+            step(functools.partial(advance_main, it))
             arrived(rest.at[pl.ds(0, lines - 1)], line_r.at[1])
             for mate in mates:
                 atoms_ref[mate] = atoms_b[0, mate, chip].astype(F32) + rest[mate].astype(F32)
@@ -340,25 +356,33 @@
             at = flipped(bits) // 2
             if bits:
                 wait_full(it, bits)
-            advance(it, 1 - core, (slice(None), at), lines)
-            give = codes_b.at[:, at, :, lanes_of(1 - core)]
-            start(copy_to(give, codes_out.at[:, at, core], 1, out_r.at[0], partner))
-            advance(it, core, (slice(None), at), lines)
-            keep = codes_b.at[:, at, :, lanes_of(core)]
-            pltpu.make_async_copy(keep, codes_out.at[:, at, core], local_sem.at[0]).start()
+            gives = ready([
+                copy_to(
+                    codes_b.at[:, at, :, lanes_of(1 - core)], codes_out.at[:, at, core], 1, out_r.at[0], partner
+                )
+            ])
+
+            @step
+            def _():
+                advance(it, 1 - core, (slice(None), at), lines)
+                gives[0].start()
+
+            @step
+            def _():
+                advance(it, core, (slice(None), at), lines)
+                held = codes_b.at[:, at, :, lanes_of(core)]
+                pltpu.make_async_copy(held, codes_out.at[:, at, core], local_sem.at[0]).start()
+
         arrived(last_recv.at[pl.ds(0, lines - 1)], sum_r.at[1])
         total = grad[group]
         for mate in mates:
             total = total + jnp.concatenate([last_recv[mate, 0], last_recv[mate, 1]], axis=1).astype(F32)
         updated = atoms_ref[group] + factor * total
-        atoms_ref[group] = updated / jnp.sqrt(jnp.mean(updated * updated, axis=1, keepdims=True) + EPSILON)
-        atoms_store = pltpu.make_async_copy(atoms_ref.at[group], atoms_out, local_sem.at[2])
-        atoms_store.start()
+        atoms_out[...] = updated / jnp.sqrt(jnp.mean(updated * updated, axis=1, keepdims=True) + EPSILON)
 
     arrived(codes_out.at[:, :, 1 - core], out_r.at[0])
     arrived(codes_out.at[:, :, core], local_sem.at[0])
-    for put in (residual_store, atoms_store):
-        put.wait()
+    residual_store.wait()
     for copy, when in sent:
         if when is None:
             copy.wait_send()
@@ -385,7 +409,7 @@
             name="learn",
             out_shape=(vmem(split, BF16), vmem(piece, F32), vmem(signal.shape, F32)),
             in_specs=[outside] * 4,
-            out_specs=(pl.BlockSpec(memory_space=pl.ANY),) * 3,
+            out_specs=[pl.BlockSpec(memory_space=space) for space in (pl.ANY, pltpu.VMEM, pl.ANY)],
             scratch_shapes=[
                 vmem((lines, *piece), F32),
                 vmem((lines, *piece), BF16),

time: 50.4 us -> 48.5 us (0.962)
  Pallas kernels: 49.6 us -> 47.7 us
    pallas_call x1, Pallas kernels: 48.6 us -> 46.7 us  [on_device(): pl.pallas_call(functools.partial(kernel, n), name='learn', out_shape=(vme...]
where the time goes in v4:
time: 48.5 us; the launch traced here: 48.4 us
  Pallas kernels  47.7 us (98%)
  between operations  0.64 us (1%)
    pallas_call x1, Pallas kernels, on_device(): pl.pallas_call(functools.partial(kernel, n), name='learn', out_shape=(vme...  46.7 us
    pallas_call x1, Pallas kernels, on_device(): pl.pallas_call(publish, name='publish', out_shape=tuple((jax.ShapeDtypeSt...  1.06 us

profile of v4, /device:TPU:0, one launch (start us, length us, event | category | flops | bytes accessed | tf_op | source)
XLA Modules:
  0.0 48.4 jit_solution(6931140126163684076)
XLA Ops:
  0.6 46.7 %learn.1 = (bf16[2,4,2,64,512]{4,3,2,1,0:T(8,128)(2,1)S(1)}, f32[64,512]{1,0:T(8,128)S(1)}, f32[1,512]{1,0:T(1,128)S(1)}) custom-call(f32[1,512]{1,0:T(1,128)} %signal_hbm.1, bf16[2,4,2,64,512]{4,3,2,1,0:T(8,128)(2,1)} %bitcast.3, f32[64,512]{1,0:T(8,128)} %dictionary_hbm.1, f32[1,1024]{1,0:T(1,128)} %bitcast.4), custom_call_target="tpu_custom_call" | custom-call | tf_op jit(solution)/shard_map/learn/pallas_call | solution.py:407
  47.3 1.1 %publish.1 = (bf16[2,4,2,64,512]{4,3,2,1,0:T(8,128)(2,1)}, f32[64,512]{1,0:T(8,128)}, f32[1,512]{1,0:T(1,128)}) custom-call(bf16[2,4,2,64,512]{4,3,2,1,0:T(8,128)(2,1)S(1)} %get-tuple-element.9.codes_ref, f32[64,512]{1,0:T(8,128)S(1)} %get-tuple-element.10.atoms_ref, f32[1,512]{1,0:T(1,128)S(1)} %get-tuple-element.11.residual_ref), custom_call_target="tpu_custom_call" | custom-call | tf_op jit(solution)/shard_map/publish/pallas_call | solution.py:458

commit v5 on v4

--- a/solution.py
+++ b/solution.py
@@ -160,7 +160,7 @@
     for mate in mates:
         held = atoms_b.at[0, group, chip]
         start(copy_to(held, held, 0, line_r.at[0], member(pos, mate)))
-    for bits in (7, 6, 3, 2, 5, 4, 1):
+    for bits in (7, 6, 5, 3, 4, 2, 1):
         at = flipped(bits)
         start(
             copy_to(
@@ -228,13 +228,13 @@
             arrived(codes_main.at[0, :, :, pl.ds(0, width)], codes_r.at[0])
             codes_main[1, :, :, pl.ds(half, width)] = codes_main[0, :, :, pl.ds(0, width)]
         atoms = atoms_b[it, :, chip].reshape(lines * rows, lag_count)
-        pair = jnp.concatenate([atoms[:, :half], atoms[:, half:]], axis=0)
+        pair = jnp.concatenate([atoms[:, :half], atoms[:, half:]], axis=0).astype(F32).T.astype(BF16)
 
         def correlate(at):
             picked = pl.ds(at, min(chunk, length - at))
             lagged[:, picked] = lax.dot_general(
                 pair, codes_main[:, :, :, picked].reshape(2 * lines * rows, picked.size),
-                (((0,), (0,)), ((), ())), preferred_element_type=F32,
+                (((1,), (0,)), ((), ())), preferred_element_type=F32,
             )
 
         correlate(0)
@@ -246,7 +246,7 @@
             if at // chunk % 2 == 0:
                 continue
             held = shares.at[it, pos, :, pl.ds(at - chunk, chunk + span.size)]
-            for bits in (7, 6, 3, 2, 5, 4, 1):
+            for bits in (7, 6, 5, 3, 4, 2, 1):
                 start(copy_to(held, held, 2, halo_r.at[it, 0], member(flipped(bits))))
             if at == chunk:
                 for to in range(team):

time: 48.5 us -> 48.5 us (level)
  no operation moved by 1% of the time
where the time goes in v5:
time: 48.5 us; the launch traced here: 48.4 us
  Pallas kernels  47.7 us (98%)
  between operations  0.64 us (1%)
    pallas_call x1, Pallas kernels, on_device(): pl.pallas_call(functools.partial(kernel, n), name='learn', out_shape=(vme...  46.7 us
    pallas_call x1, Pallas kernels, on_device(): pl.pallas_call(publish, name='publish', out_shape=tuple((jax.ShapeDtypeSt...  1.06 us

profile of v5, /device:TPU:0, one launch (start us, length us, event | category | flops | bytes accessed | tf_op | source)
XLA Modules:
  0.0 48.4 jit_solution(8412637295212549974)
XLA Ops:
  0.6 46.7 %learn.1 = (bf16[2,4,2,64,512]{4,3,2,1,0:T(8,128)(2,1)S(1)}, f32[64,512]{1,0:T(8,128)S(1)}, f32[1,512]{1,0:T(1,128)S(1)}) custom-call(f32[1,512]{1,0:T(1,128)} %signal_hbm.1, bf16[2,4,2,64,512]{4,3,2,1,0:T(8,128)(2,1)} %bitcast.3, f32[64,512]{1,0:T(8,128)} %dictionary_hbm.1, f32[1,1024]{1,0:T(1,128)} %bitcast.4), custom_call_target="tpu_custom_call" | custom-call | tf_op jit(solution)/shard_map/learn/pallas_call | solution.py:407
  47.3 1.1 %publish.1 = (bf16[2,4,2,64,512]{4,3,2,1,0:T(8,128)(2,1)}, f32[64,512]{1,0:T(8,128)}, f32[1,512]{1,0:T(1,128)}) custom-call(bf16[2,4,2,64,512]{4,3,2,1,0:T(8,128)(2,1)S(1)} %get-tuple-element.9.codes_ref, f32[64,512]{1,0:T(8,128)S(1)} %get-tuple-element.10.atoms_ref, f32[1,512]{1,0:T(1,128)S(1)} %get-tuple-element.11.residual_ref), custom_call_target="tpu_custom_call" | custom-call | tf_op jit(solution)/shard_map/publish/pallas_call | solution.py:458

commit v6 on v4

--- a/solution.py
+++ b/solution.py
@@ -152,22 +152,25 @@
     for mate in mates:
         greet(member(pos, mate))
 
+    pl.semaphore_wait(barrier, team - 1 + lines - 1)
+
+    def hand_over(bits):
+        at = flipped(bits)
+        source = codes_hbm.at[:, at // 2, at % 2]
+        start(copy_to(source, codes_main.at[0, :, :, lanes_of(pos)], 1, codes_r.at[0], member(at)))
+
+    for bits in (3, 2):
+        hand_over(bits)
     loads[0].wait()
     atoms_b[0, group, chip] = atoms_ref[group].astype(BF16)
-    rest[group] = (atoms_ref[group] - atoms_b[0, group, chip].astype(F32)).astype(BF16)
-    pl.semaphore_wait(barrier, team - 1 + lines - 1)
-
     for mate in mates:
         held = atoms_b.at[0, group, chip]
         start(copy_to(held, held, 0, line_r.at[0], member(pos, mate)))
-    for bits in (7, 6, 3, 2, 5, 4, 1):
-        at = flipped(bits)
-        start(
-            copy_to(
-                codes_hbm.at[:, at // 2, at % 2], codes_main.at[0, :, :, lanes_of(pos)], 1, codes_r.at[0], member(at)
-            )
-        )
+    for bits in (7, 6, 5, 4, 1):
+        hand_over(bits)
+    rest[group] = (atoms_ref[group] - atoms_b[0, group, chip].astype(F32)).astype(BF16)
     start(copy_to(codes_hbm.at[:, :, 1 - core], codes_b.at[:, :, :, lanes_of(core)], 1, codes_r.at[1], partner))
+
     codes_main[0, :, :, pl.ds(width, half)] = jnp.zeros((lines, rows, half), BF16)
     codes_main[1, :, :, pl.ds(0, half)] = jnp.zeros((lines, rows, half), BF16)
     loads[2].wait()

time: 48.5 us -> 48.7 us (level)
  no operation moved by 1% of the time
where the time goes in v6:
time: 48.7 us; the launch traced here: 48.5 us
  Pallas kernels  47.9 us (98%)
  between operations  0.64 us (1%)
    pallas_call x1, Pallas kernels, on_device(): pl.pallas_call(functools.partial(kernel, n), name='learn', out_shape=(vme...  46.8 us
    pallas_call x1, Pallas kernels, on_device(): pl.pallas_call(publish, name='publish', out_shape=tuple((jax.ShapeDtypeSt...  1.06 us

profile of v6, /device:TPU:0, one launch (start us, length us, event | category | flops | bytes accessed | tf_op | source)
XLA Modules:
  0.0 48.5 jit_solution(107776401238798300)
XLA Ops:
  0.6 46.8 %learn.1 = (bf16[2,4,2,64,512]{4,3,2,1,0:T(8,128)(2,1)S(1)}, f32[64,512]{1,0:T(8,128)S(1)}, f32[1,512]{1,0:T(1,128)S(1)}) custom-call(f32[1,512]{1,0:T(1,128)} %signal_hbm.1, bf16[2,4,2,64,512]{4,3,2,1,0:T(8,128)(2,1)} %bitcast.3, f32[64,512]{1,0:T(8,128)} %dictionary_hbm.1, f32[1,1024]{1,0:T(1,128)} %bitcast.4), custom_call_target="tpu_custom_call" | custom-call | tf_op jit(solution)/shard_map/learn/pallas_call | solution.py:410
  47.5 1.1 %publish.1 = (bf16[2,4,2,64,512]{4,3,2,1,0:T(8,128)(2,1)}, f32[64,512]{1,0:T(8,128)}, f32[1,512]{1,0:T(1,128)}) custom-call(bf16[2,4,2,64,512]{4,3,2,1,0:T(8,128)(2,1)S(1)} %get-tuple-element.9.codes_ref, f32[64,512]{1,0:T(8,128)S(1)} %get-tuple-element.10.atoms_ref, f32[1,512]{1,0:T(1,128)S(1)} %get-tuple-element.11.residual_ref), custom_call_target="tpu_custom_call" | custom-call | tf_op jit(solution)/shard_map/publish/pallas_call | solution.py:461
